TPU v7x, 256 devices: a whole 4x4x8 slice. The times are simulated.
256 devices in a mesh: tensor: 4 (over x_hi, core), context: 64 (over x_lo, y, z).
Axes of the slice: x: 4 (x_hi: 2, x_lo: 2; x = x_hi * 2 + x_lo), y: 4, z: 8, core: 2. Of those that a mesh axis runs over, the one named last changes fastest.
Arguments:
- query_states: bfloat16 [16384, 512], P('context', 'tensor'), may hold values from -6 to 6
- key_states: bfloat16 [16384, 512], P('context', 'tensor'), may hold values from -6 to 6
- value_states: bfloat16 [16384, 512], P('context', 'tensor'), may hold values from -6 to 6
- out_grad: bfloat16 [16384, 6144], P('context', 'tensor'), may hold values from -16 to 16
- out_proj: bfloat16 [6144, 512], P(None, 'tensor'), may hold values from -0.25 to 0.25
Outputs:
- query_grad: bfloat16 [16384, 512], P('context', 'tensor')
- key_grad: bfloat16 [16384, 512], P('context', 'tensor')
- value_grad: bfloat16 [16384, 512], P('context', 'tensor')
- proj_grad: float32 [6144, 512], P('context', 'tensor')
All inputs are finite; a program needn't handle non-finite values.
Results may differ from a plain program's by a relative error of at most 0.038.
Values may be sent and summed in bfloat16 or wider, within the bound.
A program may use at most 128 MiB of HBM per device.

v0:
```python
import math

import jax
import jax.numpy as jnp
from jax import lax
from jax.sharding import Mesh
from jax.sharding import PartitionSpec as P

HD = 128
TENSOR = ("tensor_0", "tensor_1")
CONTEXT = ("context_0", "context_1", "context_2")


log_two_e = 1.4426950408889634


def from_everyone(x, axis):
    copies = jnp.broadcast_to(x, (lax.axis_size(axis), *x.shape))
    return lax.all_to_all(copies, axis, split_axis=0, concat_axis=0, tiled=True)


def laid_out(blocks, dim):
    shape = list(blocks.shape[1:])
    shape[dim] *= blocks.shape[0]
    return jnp.moveaxis(blocks, 0, dim).reshape(shape)


def gathered_by_axis(x, axes, dim):
    far, near = axes
    blocks = from_everyone(from_everyone(x, far), near)
    return laid_out(blocks.swapaxes(0, 1).reshape(-1, *x.shape), dim)


def sent_together(arrays, axis, dim, along):
    ends, at = ([], 0)
    for a in arrays[:-1]:
        at += a.shape[along]
        ends.append(at)
    both = jnp.concatenate(arrays, axis=along)
    return tuple(jnp.split(lax.all_gather(both, axis, axis=dim, tiled=True), ends, axis=along))


def split_up(x, dim, count):
    before, after = (x.shape[:dim], x.shape[dim + 1 :])
    return jnp.moveaxis(x.reshape(*before, count, -1, *after), dim, 0)


def summed_on_arrival(x, axis, dim):
    count = lax.axis_size(axis)
    blocks = lax.all_to_all(split_up(x, dim, count), axis, 0, 0, tiled=True)
    return jnp.sum(blocks, axis=0)


def sum_in_two_steps(x, axes, dim):
    far, near = axes
    leading = summed_on_arrival(x, far, dim)
    return summed_on_arrival(leading, near, dim)


def gather_axes(x, axes, dim):
    for axis in reversed(axes):
        x = lax.all_gather(x, axis, axis=dim, tiled=True)
    return x


def by_heads(matrix):
    return matrix.reshape(matrix.shape[0], matrix.shape[1] // HD, HD)


def joined_heads(stacked):
    return jnp.transpose(stacked, (1, 0, 2)).reshape(stacked.shape[1], stacked.shape[0] * HD)


def in_blocks(update, running, members):
    row_count = members[0].shape[0]
    block_rows = math.gcd(row_count, 2048)
    stacked = tuple(
        (
            member.reshape((row_count // block_rows, block_rows) + member.shape[1:])
            for member in members
        )
    )

    def advance(running_state, portion):
        return (update(running_state, portion), None)

    result, unused = lax.scan(advance, running, stacked)
    return result


def local(query_states, key_states, value_states, out_grad, out_proj):
    scaling = HD ** (-0.5)
    score_scale = scaling * log_two_e
    features = gathered_by_axis(out_grad, ("tensor_0", "tensor_1"), 1)
    attended_grad = jnp.dot(features, out_proj, preferred_element_type=jnp.float32).astype(
        jnp.bfloat16
    )
    query_split = by_heads(query_states)
    key_split = by_heads(key_states)
    value_split = by_heads(value_states)
    grad_split = by_heads(attended_grad)
    row_count = query_split.shape[0]
    heads_here = query_split.shape[1]
    empty_heads = jnp.zeros((heads_here, row_count, HD), jnp.float32)

    def forward_block(running, members):
        row_shift, row_total, weighted = running
        key_block = by_heads(members[0])
        value_block = by_heads(members[1])
        scores = (
            jnp.einsum("qhd,khd->hqk", query_split, key_block, preferred_element_type=jnp.float32)
            * score_scale
        )
        new_shift = jnp.maximum(row_shift, jnp.ceil(jnp.max(scores, axis=2)))
        factor = jnp.exp2(row_shift - new_shift)
        powers = jnp.exp2(scores - new_shift[:, :, None])
        row_total = row_total * factor + jnp.sum(powers, axis=2)
        weighted = weighted * factor[:, :, None] + jnp.einsum(
            "hqk,khd->hqd",
            powers.astype(jnp.bfloat16),
            value_block,
            preferred_element_type=jnp.float32,
        )
        return (new_shift, row_total, weighted)

    start_state = (
        jnp.full((heads_here, row_count), -1e30, jnp.float32),
        jnp.zeros((heads_here, row_count), jnp.float32),
        empty_heads,
    )
    gathered = sent_together((key_states, value_states), CONTEXT, 0, 1)
    row_shift, row_total, weighted = in_blocks(forward_block, start_state, gathered)
    attended_heads = (weighted / row_total[:, :, None]).astype(jnp.bfloat16)
    attended = joined_heads(attended_heads)
    total_heads = row_shift + jnp.log2(row_total)
    log_total = jnp.transpose(total_heads)
    row_delta = jnp.sum(
        by_heads(attended).astype(jnp.float32) * grad_split.astype(jnp.float32), axis=2
    )
    delta_heads = jnp.transpose(row_delta)
    proj_grad = sum_in_two_steps(
        lax.dot_general(
            features, attended, (((0,), (0,)), ((), ())), preferred_element_type=jnp.float32
        ),
        ("context_0", ("context_1", "context_2")),
        0,
    )

    def query_block_grad(running, members):
        key_block = by_heads(members[0])
        value_block = by_heads(members[1])
        scores = (
            jnp.einsum("qhd,khd->hqk", query_split, key_block, preferred_element_type=jnp.float32)
            * score_scale
        )
        weights = jnp.exp2(scores - total_heads[:, :, None])
        prob_grad = jnp.einsum(
            "qhd,khd->hqk", grad_split, value_block, preferred_element_type=jnp.float32
        )
        score_grad = (weights * (prob_grad - delta_heads[:, :, None])).astype(jnp.bfloat16)
        return running + jnp.einsum(
            "hqk,khd->hqd", score_grad, key_block, preferred_element_type=jnp.float32
        )

    query_sum = in_blocks(query_block_grad, empty_heads, gathered)
    query_grad = joined_heads((query_sum * scaling).astype(jnp.bfloat16))

    def key_block_grad(running, members):
        query_block = by_heads(members[0])
        grad_block = by_heads(members[1])
        total_block = jnp.transpose(members[2])
        delta_block = jnp.transpose(members[3])
        scores = (
            jnp.einsum("qhd,khd->hqk", query_block, key_split, preferred_element_type=jnp.float32)
            * score_scale
        )
        weights = jnp.exp2(scores - total_block[:, :, None])
        prob_grad = jnp.einsum(
            "qhd,khd->hqk", grad_block, value_split, preferred_element_type=jnp.float32
        )
        score_grad = (weights * (prob_grad - delta_block[:, :, None])).astype(jnp.bfloat16)
        key_sum = running[0] + jnp.einsum(
            "hqk,qhd->hkd", score_grad, query_block, preferred_element_type=jnp.float32
        )
        value_sum = running[1] + jnp.einsum(
            "hqk,qhd->hkd",
            weights.astype(jnp.bfloat16),
            grad_block,
            preferred_element_type=jnp.float32,
        )
        return (key_sum, value_sum)

    key_sum, value_sum = in_blocks(
        key_block_grad,
        (empty_heads, empty_heads),
        (
            gather_axes(
                query_states.astype(jnp.float32), ("context_2", "context_1", "context_0"), 0
            ).astype(jnp.bfloat16),
            gather_axes(
                attended_grad.astype(jnp.float32), ("context_2", "context_1", "context_0"), 0
            ).astype(jnp.bfloat16),
            gather_axes(log_total, ("context_2", "context_1", "context_0"), 0),
            gather_axes(row_delta, ("context_2", "context_1", "context_0"), 0),
        ),
    )
    key_grad = joined_heads((key_sum * scaling).astype(jnp.bfloat16))
    value_grad = joined_heads(value_sum.astype(jnp.bfloat16))
    return (query_grad, key_grad, value_grad, proj_grad)


def solution(mesh):
    torus = Mesh(
        mesh.devices.reshape(2, 2, 2, 4, 8),
        ("tensor_0", "tensor_1", "context_0", "context_1", "context_2"),
    )
    placed = (
        P(CONTEXT, TENSOR),
        P(CONTEXT, TENSOR),
        P(CONTEXT, TENSOR),
        P(CONTEXT, TENSOR),
        P(None, TENSOR),
    )
    return jax.shard_map(
        local,
        mesh=torus,
        in_specs=placed,
        out_specs=(P(CONTEXT, TENSOR), P(CONTEXT, TENSOR), P(CONTEXT, TENSOR), P(CONTEXT, TENSOR)),
        check_vma=False,
    )
```

profile of v0, /device:TPU:8, one launch (start us, length us, event | category | flops | bytes accessed | tf_op | source)
XLA Modules:
  0.0 664.9 jit_solution(16566410237212033508)
XLA Ops:
  11.3 4.3 all-to-all-start
  15.6 20.7 %all-to-all-done = bf16[2,256,1536]{2,1,0:T(8,128)(2,1)S(1)} async-done(((bf16[2,256,1536]{2,1,0:T(8,128)(2,1)}), bf16[2,256,1536]{2,1,0:T(8,128)(2,1)S(1)}, u32[]{:S(2)}, u32[]{:S(2)}) %all-to-all-start) | async-done | bytes 1572896 | tf_op jit(solution)/shard_map/all_to_all | solution.py:19
  36.6 6.3 all_to_all.20
  44.8 4.7 copy.24
  49.4 264.1 %all-gather.12.cloned.1.call-done = bf16[16384,256]{1,0:T(8,128)(2,1)} async-done(((bf16[256,256]{1,0:T(8,128)(2,1)}), bf16[16384,256]{1,0:T(8,128)(2,1)}) %all-gather.12.cloned.1.call-update) | async-done | bytes 8388624 | tf_op jit(solution)/shard_map/all_gather | solution.py:40
  313.6 5.7 fusion.73
  319.3 53.0 %while.39 = (s32[]{:T(128)}, f32[1,256]{1,0:T(1,128)S(1)}, f32[1,256]{1,0:T(1,128)S(1)}, f32[1,256,128]{2,1,0:T(8,128)S(1)}, bf16[8,2048,128]{2,1,0:T(8,128)(2,1...) while((s32[]{:T(128)}, f32[1,256]{1,0:T(1,128)S(1)}, ...), condition=%wide.region_3.4_spmd.clone, body=%wide.region_0.3_spmd.clone.sunk | while | flops 272729856 | bytes 16074901 | solution.py:87
  325.9 2.8 fusion.103
  375.1 4.9 all_gather.46
  380.1 21.7 %all_gather.47 = bf16[2048,128]{0,1:T(8,128)(2,1)} all-gather(bf16[512,128]{0,1:T(8,128)(2,1)S(1)} %all_gather.46), channel_id=1, replica_groups=mesh['tensor_0'=2,'tensor_1'=2,'context_0'=2,'context_1'=4,'context_2'=8..., dimensions={0}, use_global_device_ids=true | all-gather | bytes 655360 | tf_op jit(solution)/shard_map/all_gather | solution.py:62
  401.9 4.9 all_gather.40
  406.8 13.5 %all_gather.41 = bf16[2048,128]{1,0:T(8,128)(2,1)} all-gather(bf16[512,128]{1,0:T(8,128)(2,1)S(1)} %all_gather.40), channel_id=1, replica_groups=mesh['tensor_0'=2,'tensor_1'=2,'context_0'=2,'context_1'=4,'context_2'=8..., dimensions={0}, use_global_device_ids=true | all-gather | bytes 655360 | tf_op jit(solution)/shard_map/all_gather | solution.py:62
  420.3 3.1 fusion.70
  425.3 5.2 all-to-all-start.2
  430.7 20.5 %all-gather = f32[1,512]{1,0:T(1,128)S(1)} all-gather(f32[1,256]{1,0:T(1,128)S(1)} %multiply_add_fusion), channel_id=2, replica_groups=mesh['tensor_0'=2,'tensor_1'=2,'context_0'=2,'context_1'=4,'context_2'=8..., dimensions={1}, use_global_device_ids=true | all-gather | bytes 3072 | tf_op jit(solution)/shard_map/all_gather | solution.py:62
  451.3 4.2 all-gather.6
  455.5 11.7 %all-gather.1 = f32[1,2048]{1,0:T(1,128)S(1)} all-gather(f32[1,512]{1,0:T(1,128)S(1)} %all-gather), channel_id=3, replica_groups=mesh['tensor_0'=2,'tensor_1'=2,'context_0'=2,'context_1'=4,'context_2'=8..., dimensions={1}, use_global_device_ids=true | all-gather | bytes 10240 | tf_op jit(solution)/shard_map/all_gather | solution.py:62
  467.2 10.4 %all-gather.7 = f32[4,1,512]{2,1,0:T(1,128)S(1)} all-gather(f32[1,1,512]{2,1,0:T(1,128)S(1)} %bitcast.193), channel_id=6, replica_groups=mesh['tensor_0'=2,'tensor_1'=2,'context_0'=2,'context_1'=4,'context_2'=8..., dimensions={0}, use_global_device_ids=true | all-gather | bytes 10240 | tf_op jit(solution)/shard_map/all_gather | solution.py:62
  477.6 26.0 %all-gather.2 = f32[1,16384]{1,0:T(1,128)S(1)} all-gather(f32[1,2048]{1,0:T(1,128)S(1)} %all-gather.1), channel_id=4, replica_groups=mesh['tensor_0'=2,'tensor_1'=2,'context_0'=2,'context_1'=4,'context_2'=8..., dimensions={1}, use_global_device_ids=true | all-gather | bytes 73728 | tf_op jit(solution)/shard_map/all_gather | solution.py:62
  503.6 24.6 %all-gather.5 = f32[16384]{0:T(1024)S(1)} all-gather(f32[2048]{0:T(1024)S(1)} %bitcast.192), channel_id=7, replica_groups=mesh['tensor_0'=2,'tensor_1'=2,'context_0'=2,'context_1'=4,'context_2'=8..., dimensions={0}, use_global_device_ids=true | all-gather | bytes 73728 | tf_op jit(solution)/shard_map/all_gather | solution.py:62
  532.1 6.7 %all-to-all-start.3 = ((f32[32,96,128]{2,1,0:T(8,128)}), f32[32,96,128]{2,1,0:T(8,128)S(1)}, u32[]{:S(2)}, u32[]{:S(2)}) async-start(f32[32,96,128]{2,1,0:T(8,128)} %bitcast.24), calls=%async_computation.3 | async-start | bytes 3145728 | tf_op jit(solution)/shard_map/all_to_all | solution.py:50
  538.8 45.9 %while.40 = (s32[]{:T(128)}, f32[1,256,128]{2,1,0:T(8,128)S(1)}, bf16[8,2048,128]{2,1,0:T(8,128)(2,1)}, bf16[256,1,128]{2,0,1:T(8,128)(2,1)S(1)}, f32[1,256]{1,0...) while((s32[]{:T(128)}, f32[1,256,128]{2,1,0:T(8,128)S(1)}, ...), condition=%wide.region_6.7_spmd.clone, body=%wide.region_5.6_spmd.clone.sunk | while | flops 405864448 | bytes 6164090 | solution.py:87
  538.8 3.0 fusion.113
  544.5 3.0 fusion.113
  550.3 3.0 fusion.113
  556.0 3.0 fusion.113
  561.8 3.0 fusion.113
  567.5 3.0 fusion.113
  573.2 3.0 fusion.113
  579.0 3.0 fusion.113
  586.1 6.4 copy.31
  592.5 64.4 %while.41 = (s32[]{:T(128)}, f32[1,256,128]{2,1,0:T(8,128)S(1)}, f32[1,256,128]{2,1,0:T(8,128)S(1)}, bf16[8,2048,128]{2,1,0:T(8,128)(2,1)}, bf16[256,1,128]{2,0,...) while((s32[]{:T(128)}, f32[1,256,128]{2,1,0:T(8,128)S(1)}, ...), condition=%wide.region_8.9_spmd.clone, body=%wide.region_7.8_spmd.clone.sunk | while | flops 540672000 | bytes 9094795 | solution.py:87
  592.5 3.0 fusion.122
  595.5 2.8 fusion.123
  600.6 3.0 fusion.122
  603.6 2.8 fusion.123
  608.6 3.0 fusion.122
  611.6 2.8 fusion.123
  616.7 3.0 fusion.122
  619.7 2.8 fusion.123
  624.8 3.0 fusion.122
  627.7 2.8 fusion.123
  632.8 3.0 fusion.122
  635.8 2.8 fusion.123
  640.9 3.0 fusion.122
  643.9 2.8 fusion.123
  648.9 3.0 fusion.122
  651.9 2.8 fusion.123
  (135 shorter events, 107.6 us)
Async XLA Ops:
  7.2 365.3 %copy-start = (bf16[6144,128]{1,0:T(8,128)(2,1)S(1)}, bf16[6144,128]{1,0:T(8,128)(2,1)}, u32[]{:S(2)}) copy-start(bf16[6144,128]{1,0:T(8,128)(2,1)} %param.15) | copy-start | bytes 4718596
  7.2 306.4 %all-gather.12.cloned.1.call-start = ((), (), s32[]{:S(2)}) async-start(), calls=%async_computation.4 | async-start | bytes 8519680 | tf_op jit(solution)/shard_map/all_gather | solution.py:40
  11.3 25.0 %all-to-all-start = ((bf16[2,256,1536]{2,1,0:T(8,128)(2,1)}), bf16[2,256,1536]{2,1,0:T(8,128)(2,1)S(1)}, u32[]{:S(2)}, u32[]{:S(2)}) async-start(bf16[2,256,1536]{2,1,0:T(8,128)(2,1)} %broadcast_in_dim.22), calls=%async_computation | async-start | bytes 3145728 | tf_op jit(solution)/shard_map/all_to_all | solution.py:19
  15.6 570.4 %all-gather.16.cloned.1.call-start = ((), (), s32[]{:S(2)}) async-start(), calls=%async_computation.6 | async-start | bytes 4718592 | tf_op jit(solution)/shard_map/all_gather | solution.py:62
  49.4 269.8 %copy-start.3 = (bf16[256,128]{1,0:T(8,128)(2,1)S(1)}, bf16[256,128]{1,0:T(8,128)(2,1)}, u32[]{:S(2)}) copy-start(bf16[256,128]{1,0:T(8,128)(2,1)} %param.11) | copy-start | bytes 196612
  322.1 2.2 copy-start.2
  328.7 2.2 copy-start.2
  335.3 2.2 copy-start.2
  342.0 2.2 copy-start.2
  348.6 2.2 copy-start.2
  355.2 2.2 copy-start.2
  361.9 2.2 copy-start.2
  368.5 2.2 copy-start.2
  401.8 190.7 %all-gather.14.cloned.1.call-start = ((), (), s32[]{:S(2)}) async-start(), calls=%async_computation.5 | async-start | bytes 4718592 | tf_op jit(solution)/shard_map/all_gather | solution.py:62
  425.3 102.8 %all-to-all-start.2 = ((f32[2,3072,128]{1,2,0:T(8,128)}), f32[2,3072,128]{1,2,0:T(8,128)}, u32[]{:S(2)}, u32[]{:S(2)}) async-start(f32[2,3072,128]{1,2,0:T(8,128)} %bitcast.166), calls=%async_computation.2 | async-start | bytes 6291456 | tf_op jit(solution)/shard_map/all_to_all | solution.py:50
  532.1 53.3 %all-to-all-start.3 = ((f32[32,96,128]{2,1,0:T(8,128)}), f32[32,96,128]{2,1,0:T(8,128)S(1)}, u32[]{:S(2)}, u32[]{:S(2)}) async-start(f32[32,96,128]{2,1,0:T(8,128)} %bitcast.24), calls=%async_computation.3 | async-start | bytes 3145728 | tf_op jit(solution)/shard_map/all_to_all | solution.py:50
  586.1 6.4 copy-start.4
  586.1 6.4 copy-start.5
  657.0 1.5 copy-start.1
Sparse Core Ops, SparseCore 0:
  9.8 303.6 all-gather.11
  401.9 55.1 all-gather.15
  459.0 70.9 all-gather.13
where the time goes:
time: 668 us; the launch traced here: 665 us
  waiting for transfers between devices  285 us (43%)
  matrix products  151 us (23%)
  blocking collectives  149 us (22%)
  local copies, waits for them, and re-layouts  26.2 us (4%)
  other arithmetic  23.5 us (4%)
  starting transfers between devices  16.3 us (2%)
  between operations  13.9 us (2%)
    all_gather x1, waiting for transfers between devices, sent_together(): lax.all_gather(both, axis, axis=dim, tiled=True)  264 us
    all_gather x10, blocking collectives, gather_axes(): x = lax.all_gather(x, axis, axis=dim, tiled=True)  143 us
    dot_general x8, matrix products, key_block_grad(): jnp.einsum('qhd,khd->hqk', query_block, key_split, preferred_element_type...  23.9 us
    dot_general x8, matrix products, query_block_grad(): jnp.einsum('qhd,khd->hqk', query_split, key_block, preferred_element_type...  23.6 us
    dot_general x8, matrix products, key_block_grad(): jnp.einsum('hqk,qhd->hkd', score_grad, query_block, preferred_element_typ...  22.7 us
    dot_general x8, matrix products, forward_block(): jnp.einsum('qhd,khd->hqk', query_split, key_block, preferred_element_type...  22.5 us
    dot_general x8, matrix products, query_block_grad(): jnp.einsum('hqk,khd->hqd', score_grad, key_block, preferred_element_type=...  22.1 us
    all_to_all x1, waiting for transfers between devices, from_everyone(): return lax.all_to_all(copies, axis, split_axis=0, concat_axis=0, tiled=True)  20.7 us
  transfers between devices with their start and end apart: 6, of which 2 were waited for; matrix products, arithmetic and copies ran while one was open for 11% of the time, Pallas kernels for 0%

commit v1 on v0

v1 whole, which is shorter than its diff:
```python
import jax
import jax.numpy as jnp
from jax import lax
from jax.experimental import pallas as pl
from jax.experimental.pallas import tpu as pltpu
from jax.sharding import Mesh
from jax.sharding import PartitionSpec as P

HD = 128
ROWS = 256
TENSOR = ("tensor_0", "tensor_1")
CONTEXT = ("context_0", "context_1", "context_2")
SCALING = HD ** (-0.5)
SCORE_SCALE = SCALING * 1.4426950408889634
FEATURES = 1536
HALF = FEATURES // 2
PIECE = HALF // 8

BF16 = jnp.bfloat16
F32 = jnp.float32

(Q, K, V, G, O, L, ST, DQ, DK, DV, W, PA, A, S1, S2) = range(15)


def dot(a, b, ca, cb):
    return lax.dot_general(a, b, (((ca,), (cb,)), ((), ())), preferred_element_type=F32)


def fold(x, op):
    return op(x.reshape(x.shape[0] // 8, 8, x.shape[1]), axis=0)


def z_offset(i):
    odd = lax.rem(i, 2)
    return odd * lax.div(i + 1, 2) + (1 - odd) * lax.rem(8 - lax.div(i, 2), 8)


def kernel(
    q_in, k_in, v_in, og_in, w_in,
    dq_out, dk_out, dv_out, dw_out,
    qg, kg, vg, kt, vt, og, ogt, wg, part, part_in, gt, gs,
    s_tile, powers, grads, shift,
    o_send, o_in, l_send, l_in, st_send, st_in,
    att, dq_send, dq_in, dk_send, dk_in, dv_send, dv_in,
    s1_send, s1_in, s2_send, s2_in,
    send, recv, here,
):
    xh = lax.axis_index("tensor_0")
    co = lax.axis_index("tensor_1")
    xl = lax.axis_index("context_0")
    y = lax.axis_index("context_1")
    z = lax.axis_index("context_2")

    def z_to(i):
        return {"context_2": lax.rem(z + z_offset(i), 8)}

    def z_back(i):
        return {"context_2": lax.rem(z + 8 - z_offset(i), 8)}

    def u_to(e):
        return {
            "context_0": lax.rem(xl + lax.div(e, 4), 2),
            "context_1": lax.rem(y + lax.rem(e, 4), 4),
        }

    def u_back(e):
        return {
            "context_0": lax.rem(xl + lax.div(e, 4), 2),
            "context_1": lax.rem(y + 4 - lax.rem(e, 4), 4),
        }

    def t_to(s):
        return {
            "tensor_0": lax.rem(xh + s // 2, 2),
            "tensor_1": lax.rem(co + s % 2, 2),
        }

    def w_to(s):
        target = t_to(s)
        if s // 2:
            target["context_0"] = 1 - xl
        return target

    t_is_u = jnp.logical_and(xl == xh, lax.div(y, 2) == co)

    def s2_to(i):
        return {
            "tensor_0": xl,
            "tensor_1": lax.div(y, 2),
            "context_0": xh,
            "context_1": 2 * co + lax.rem(y, 2),
            "context_2": lax.rem(z + z_offset(i), 8),
        }

    def remote(src, dst, row, slot, target):
        return pltpu.make_async_remote_copy(
            src_ref=src,
            dst_ref=dst,
            send_sem=send.at[row, slot],
            recv_sem=recv.at[row, slot],
            device_id=target,
            device_id_type=pl.DeviceIdType.MESH,
        )

    def rows(ref, e, count=ROWS):
        return ref.at[pl.ds(e * count, count)]

    tensor_place = 2 * xh + co
    local = [
        pltpu.make_async_copy(q_in, rows(qg, 0), here.at[0]),
        pltpu.make_async_copy(k_in, rows(kg, 0), here.at[1]),
        pltpu.make_async_copy(v_in, rows(vg, 0), here.at[2]),
        pltpu.make_async_copy(og_in, og, here.at[3]),
        pltpu.make_async_copy(
            w_in.at[pl.ds(pl.multiple_of(tensor_place * FEATURES, FEATURES), FEATURES)],
            wg.at[0],
            here.at[4],
        ),
    ]
    for copy in local:
        copy.start()

    barrier = pltpu.get_barrier_semaphore()

    def greet(target):
        pl.semaphore_signal(
            barrier, inc=1, device_id=target, device_id_type=pl.DeviceIdType.MESH
        )

    for i in range(1, 8):
        greet(z_to(i))
        greet(u_to(i))
        greet(s2_to(i))
    for s in range(1, 4):
        greet(t_to(s))
    for s in range(2, 4):
        greet(w_to(s))

    @pl.when(jnp.logical_not(t_is_u))
    def _():
        greet(s2_to(0))
        pl.semaphore_wait(barrier, 27)

    @pl.when(t_is_u)
    def _():
        pl.semaphore_wait(barrier, 26)

    def q_copy(i):
        return remote(q_in, rows(qg, i), Q, i, z_to(i))

    def k_copy(e):
        return remote(k_in, rows(kg, e), K, e, u_to(e))

    def v_copy(e):
        return remote(v_in, rows(vg, e), V, e, u_to(e))

    def w_copy(s):
        place = 2 * lax.rem(xh + s // 2, 2) + lax.rem(co + s % 2, 2)
        block = w_in.at[pl.ds(pl.multiple_of(place * FEATURES, FEATURES), FEATURES)]
        return remote(block, wg.at[s], W, s, w_to(s))

    near = (1, 3, 4, 5, 7, 2, 6)
    for i, e in enumerate(near):
        k_copy(e).start()
        q_copy(i + 1).start()
    for s in (1, 2, 3):
        w_copy(s).start()
    for e in near:
        v_copy(e).start()
    for copy in local:
        copy.wait()

    for c in range(FEATURES // ROWS):
        ogt[c * ROWS : (c + 1) * ROWS, :] = (
            og[:, c * ROWS : (c + 1) * ROWS].astype(F32).T.astype(BF16)
        )

    for e in (0,) + near:
        if e:
            k_copy(e).wait_recv()
        kt[:, e * ROWS : (e + 1) * ROWS] = kg[e * ROWS : (e + 1) * ROWS, :].astype(F32).T.astype(BF16)
    for e in (0,) + near:
        if e:
            v_copy(e).wait_recv()
        vt[:, e * ROWS : (e + 1) * ROWS] = vg[e * ROWS : (e + 1) * ROWS, :].astype(F32).T.astype(BF16)

    def o_copy(i):
        return remote(o_send.at[i], o_in.at[i], O, i, z_back(i))

    def l_copy(i):
        return remote(l_send.at[i], l_in.at[i], L, i, z_back(i))

    def forward(i, unused):
        @pl.when(i > 0)
        def _():
            q_copy(i).wait_recv()

        lanes = pl.ds(pl.multiple_of(i * ROWS, ROWS), ROWS)
        q_block = qg[lanes, :]
        top = None
        for j in range(8):
            part_rows = slice(j * ROWS, (j + 1) * ROWS)
            scores = dot(kg[part_rows, :], q_block, 1, 1) * SCORE_SCALE
            s_tile[part_rows, :] = scores
            highest = fold(scores, jnp.max)
            top = highest if top is None else jnp.maximum(top, highest)
        row_shift = jnp.ceil(jnp.max(top, axis=0, keepdims=True))
        shift[i] = row_shift
        total = jnp.zeros((8, ROWS), F32)
        weighted = jnp.zeros((HD, ROWS), F32)
        for j in range(8):
            part_rows = slice(j * ROWS, (j + 1) * ROWS)
            p = jnp.exp2(s_tile[part_rows, :] - row_shift)
            total = total + fold(p, jnp.sum)
            p = p.astype(BF16)
            powers[part_rows, lanes] = p
            weighted = weighted + dot(vt[:, part_rows], p, 1, 0)
        row_total = jnp.sum(total, axis=0, keepdims=True)
        o_send[i] = (weighted / row_total).astype(BF16)
        l_send[i] = jnp.broadcast_to(row_shift + jnp.log2(row_total), (8, ROWS))

        @pl.when(i > 0)
        def _():
            o_copy(i).start()
            l_copy(i).start()

        return unused

    lax.fori_loop(0, 8, forward, 0)

    def part_copy(s):
        return remote(part.at[s], part_in.at[s], PA, s, t_to(s))

    for s in (2, 3, 1):
        w_copy(s).wait_recv()
        part[s] = dot(og[...], wg[s], 1, 0).astype(BF16)
        part_copy(s).start()
    g_sum = dot(og[...], wg[0], 1, 0)
    for s in (1, 2, 3):
        part_copy(s).wait_recv()
        g_sum = g_sum + part_in[s].astype(F32)
    g_own = g_sum.T.astype(BF16)
    gt[0] = g_own

    def g_copy(i):
        return remote(gt.at[0], gt.at[i], G, i, z_to(i))

    for i in range(1, 8):
        g_copy(i).start()

    for i in range(1, 8):
        l_copy(i).wait_recv()
    log_parts = [l_send[0][0:1, :]] + [l_in[i][0:1, :] for i in range(1, 8)]
    highest = log_parts[0]
    for value in log_parts[1:]:
        highest = jnp.maximum(highest, value)
    factors = [jnp.exp2(value - highest) for value in log_parts]
    total = factors[0]
    for value in factors[1:]:
        total = total + value
    joined = (factors[0] / total) * o_send[0].astype(F32)
    for i in range(1, 8):
        o_copy(i).wait_recv()
        joined = joined + (factors[i] / total) * o_in[i].astype(F32)
    attended = joined.astype(BF16)
    att[0] = attended

    def a_copy(s):
        return remote(att.at[0], att.at[s], A, s, t_to(s))

    for s in (2, 3, 1):
        a_copy(s).start()

    log_total = highest + jnp.log2(total)
    row_delta = jnp.sum(attended.astype(F32) * g_own.astype(F32), axis=0, keepdims=True)
    st_send[0:8, :] = jnp.broadcast_to(log_total, (8, ROWS))
    st_send[8:16, :] = jnp.broadcast_to(row_delta, (8, ROWS))
    st_in[0] = st_send[...]

    def st_copy(i):
        return remote(st_send, st_in.at[i], ST, i, z_to(i))

    for i in range(1, 8):
        st_copy(i).start()

    def s1_copy(e):
        return remote(s1_send.at[e], s1_in.at[e], S1, e, u_to(e))

    for s in (1, 2, 3):
        a_copy(s).wait_recv()

    def project(e, unused):
        u = u_to(e)
        head_hi, head_lo = u["context_0"], lax.div(u["context_1"], 2)
        half = lax.rem(u["context_1"], 2)
        place = 2 * lax.rem(head_hi + xh, 2) + lax.rem(head_lo + co, 2)
        block = ogt[pl.ds(pl.multiple_of(half * HALF, HALF), HALF), :]
        s1_send[e] = dot(block, att[place], 1, 1).astype(BF16)

        @pl.when(e > 0)
        def _():
            s1_copy(e).start()

        return unused

    lax.fori_loop(0, 8, project, 0)

    def dq_copy(i):
        return remote(dq_send.at[i], dq_in.at[i], DQ, i, z_back(i))

    def backward(i, unused):
        @pl.when(i > 0)
        def _():
            g_copy(i).wait_recv()
            st_copy(i).wait_recv()

        lanes = pl.ds(pl.multiple_of(i * ROWS, ROWS), ROWS)
        factor = jnp.exp2(shift[i] - st_in[i, 0:1, :])
        delta = factor * st_in[i, 8:9, :]
        g_block = (gt[i].astype(F32) * factor).astype(BF16)
        gs[:, lanes] = g_block
        query_sum = jnp.zeros((HD, ROWS), F32)
        for j in range(8):
            part_rows = slice(j * ROWS, (j + 1) * ROWS)
            prob = dot(vg[part_rows, :], g_block, 1, 0)
            score = ((prob - delta) * powers[part_rows, lanes].astype(F32)).astype(BF16)
            grads[part_rows, lanes] = score
            query_sum = query_sum + dot(kt[:, part_rows], score, 1, 0)
        dq_send[i] = query_sum.astype(BF16)

        @pl.when(i > 0)
        def _():
            dq_copy(i).start()

        return unused

    lax.fori_loop(0, 8, backward, 0)

    def dk_copy(e):
        return remote(dk_send.at[e], dk_in.at[e], DK, e, u_back(e))

    def dv_copy(e):
        return remote(dv_send.at[e], dv_in.at[e], DV, e, u_back(e))

    def key_side(n, unused):
        e = lax.rem(n + 1, 8)
        part_rows = pl.ds(pl.multiple_of(e * ROWS, ROWS), ROWS)
        dk_send[e] = dot(grads[part_rows, :], qg[...], 1, 0).astype(BF16)

        @pl.when(e > 0)
        def _():
            dk_copy(e).start()

        dv_send[e] = dot(powers[part_rows, :], gs[...], 1, 1).astype(BF16)

        @pl.when(e > 0)
        def _():
            dv_copy(e).start()

        return unused

    lax.fori_loop(0, 8, key_side, 0)

    for e in range(1, 8):
        s1_copy(e).wait_recv()
    for c in range(8):
        piece = slice(c * PIECE, (c + 1) * PIECE)
        acc = s1_send[0, piece, :].astype(F32)
        for e in range(1, 8):
            acc = acc + s1_in[e, piece, :].astype(F32)
        s2_send[c] = acc.astype(BF16)

    def s2_copy(i):
        return remote(
            s2_send.at[lax.rem(z + z_offset(i), 8)], s2_in.at[i], S2, i, s2_to(i)
        )

    for i in range(1, 8):
        s2_copy(i).start()

    @pl.when(jnp.logical_not(t_is_u))
    def _():
        s2_copy(0).start()

    @pl.when(t_is_u)
    def _():
        s2_in[0] = s2_send[z]

    acc = dq_send[0].astype(F32)
    for i in range(1, 8):
        dq_copy(i).wait_recv()
        acc = acc + dq_in[i].astype(F32)
    dq_out[...] = (acc * SCALING).T.astype(BF16)
    acc = dk_send[0].astype(F32)
    for e in range(1, 8):
        dk_copy(e).wait_recv()
        acc = acc + dk_in[e].astype(F32)
    dk_out[...] = (acc * SCALING).astype(BF16)
    acc = dv_send[0].astype(F32)
    for e in range(1, 8):
        dv_copy(e).wait_recv()
        acc = acc + dv_in[e].astype(F32)
    dv_out[...] = acc.astype(BF16)

    @pl.when(jnp.logical_not(t_is_u))
    def _():
        s2_copy(0).wait_recv()

    acc = s2_in[0].astype(F32)
    for i in range(1, 8):
        s2_copy(i).wait_recv()
        acc = acc + s2_in[i].astype(F32)
    dw_out[...] = acc

    for i in range(1, 8):
        for copy in (q_copy, k_copy, v_copy, g_copy, o_copy, l_copy, st_copy, dq_copy, dk_copy,
                     dv_copy, s1_copy, s2_copy):
            copy(i).wait_send()
    for s in range(1, 4):
        for copy in (w_copy, part_copy, a_copy):
            copy(s).wait_send()

    @pl.when(jnp.logical_not(t_is_u))
    def _():
        s2_copy(0).wait_send()


def local(q, k, v, og, w):
    anywhere = pl.BlockSpec(memory_space=pl.ANY)
    vmem = pl.BlockSpec(memory_space=pltpu.VMEM)
    tokens = 8 * ROWS
    block = (8, ROWS, HD)
    turned = (8, HD, ROWS)
    return pl.pallas_call(
        kernel,
        out_shape=(
            jax.ShapeDtypeStruct((ROWS, HD), BF16),
            jax.ShapeDtypeStruct((ROWS, HD), BF16),
            jax.ShapeDtypeStruct((ROWS, HD), BF16),
            jax.ShapeDtypeStruct((PIECE, HD), F32),
        ),
        in_specs=[anywhere] * 5,
        out_specs=(vmem,) * 4,
        scratch_shapes=[
            pltpu.VMEM((tokens, HD), BF16),
            pltpu.VMEM((tokens, HD), BF16),
            pltpu.VMEM((tokens, HD), BF16),
            pltpu.VMEM((HD, tokens), BF16),
            pltpu.VMEM((HD, tokens), BF16),
            pltpu.VMEM((ROWS, FEATURES), BF16),
            pltpu.VMEM((FEATURES, ROWS), BF16),
            pltpu.VMEM((4, FEATURES, HD), BF16),
            pltpu.VMEM((4, ROWS, HD), BF16),
            pltpu.VMEM((4, ROWS, HD), BF16),
            pltpu.VMEM(turned, BF16),
            pltpu.VMEM((HD, tokens), BF16),
            pltpu.VMEM((tokens, ROWS), F32),
            pltpu.VMEM((tokens, tokens), BF16),
            pltpu.VMEM((tokens, tokens), BF16),
            pltpu.VMEM((8, 1, ROWS), F32),
            pltpu.VMEM(turned, BF16),
            pltpu.VMEM(turned, BF16),
            pltpu.VMEM((8, 8, ROWS), F32),
            pltpu.VMEM((8, 8, ROWS), F32),
            pltpu.VMEM((16, ROWS), F32),
            pltpu.VMEM((8, 16, ROWS), F32),
            pltpu.VMEM((4, HD, ROWS), BF16),
            pltpu.VMEM(turned, BF16),
            pltpu.VMEM(turned, BF16),
            pltpu.VMEM(block, BF16),
            pltpu.VMEM(block, BF16),
            pltpu.VMEM(block, BF16),
            pltpu.VMEM(block, BF16),
            pltpu.VMEM((8, HALF, HD), BF16),
            pltpu.VMEM((8, HALF, HD), BF16),
            pltpu.VMEM((8, PIECE, HD), BF16),
            pltpu.VMEM((8, PIECE, HD), BF16),
            pltpu.SemaphoreType.DMA((15, 8)),
            pltpu.SemaphoreType.DMA((15, 8)),
            pltpu.SemaphoreType.DMA((5,)),
        ],
        compiler_params=pltpu.CompilerParams(
            collective_id=0,
            has_side_effects=True,
            vmem_limit_bytes=56 * 1024 * 1024,
        ),
    )(q, k, v, og, w)


def solution(mesh):
    torus = Mesh(mesh.devices.reshape(2, 2, 2, 4, 8), TENSOR + CONTEXT)
    tiles = P(CONTEXT, TENSOR)
    return jax.shard_map(
        local,
        mesh=torus,
        in_specs=(tiles, tiles, tiles, tiles, P(None, TENSOR)),
        out_specs=(tiles, tiles, tiles, tiles),
        check_vma=False,
    )
```

time: 668 us -> 96.6 us (0.14)
  the two profiles are of different devices: /device:TPU:8 before, /device:TPU:1 now
where the time goes in v1:
time: 96.6 us; the launch traced here: 96.4 us
  Pallas kernels  89.9 us (93%)
  local copies, waits for them, and re-layouts  5.84 us (6%)
    pallas_call x1, Pallas kernels, local(): pl.pallas_call(kernel, out_shape=(jax.ShapeDtypeStruct((ROWS, HD), BF16),...  89.9 us
    unnamed x4, local copies, waits for them, and re-layouts  5.84 us

profile of v1, /device:TPU:1, one launch (start us, length us, event | category | flops | bytes accessed | tf_op | source)
XLA Modules:
  0.0 96.4 jit_solution(4326317824963598873)
XLA Ops:
  0.6 89.9 %shard_map.84 = (bf16[256,128]{1,0:T(8,128)(2,1)}, bf16[256,128]{1,0:T(8,128)(2,1)}, bf16[256,128]{1,0:T(8,128)(2,1)}, f32[96,128]{1,0:T(8,128)}) custom-call(bf16[256,128]{1,0:T(8,128)(2,1)} %q_in.1, bf16[256,128]{1,0:T(8,128)(2,1)} %k_in.1, bf16[256,128]{1,0:T(8,128)(2,1)} %v_in.1, bf16[256,1536]{1,0:T(8,128)(2,1)} %og_in.1, bf16[6144,128]{1,0:T(8,128)(2,1)} %w_in.1), custom_call_target="tpu_custom_call" | custom-call | tf_op jit(solution)/shard_map/pallas_call | solution.py:434
  90.5 1.5 %copy.13 = bf16[256,128]{1,0:T(8,128)(2,1)} copy(bf16[256,128]{1,0:T(8,128)(2,1)} %get-tuple-element.8) | data formatting | bytes 131072
  92.0 1.5 %copy.14 = bf16[256,128]{1,0:T(8,128)(2,1)} copy(bf16[256,128]{1,0:T(8,128)(2,1)} %get-tuple-element.9) | data formatting | bytes 131072
  93.5 1.5 %copy.15 = bf16[256,128]{1,0:T(8,128)(2,1)} copy(bf16[256,128]{1,0:T(8,128)(2,1)} %get-tuple-element.10) | data formatting | bytes 131072
  95.0 1.4 %copy.16 = f32[96,128]{1,0:T(8,128)} copy(f32[96,128]{1,0:T(8,128)} %get-tuple-element.11) | data formatting | bytes 98304

commit v2 on v1

v2 whole, which is shorter than its diff:
```python
import jax
import jax.numpy as jnp
from jax import lax
from jax.experimental import pallas as pl
from jax.experimental.pallas import tpu as pltpu
from jax.sharding import Mesh
from jax.sharding import PartitionSpec as P

HD = 128
ROWS = 256
TENSOR = ("tensor_0", "tensor_1")
CONTEXT = ("context_0", "context_1", "context_2")
SCALING = HD ** (-0.5)
SCORE_SCALE = SCALING * 1.4426950408889634
FEATURES = 1536
PIECE = 96

BF16 = jnp.bfloat16
F32 = jnp.float32

(Q, K, V, G, O, L, ST, DQ, DK, DV, W, PA, X, XC, AT, AC, S2) = range(17)
EARLY = 6
SUBSET = 192


def dot(a, b, ca, cb):
    return lax.dot_general(a, b, (((ca,), (cb,)), ((), ())), preferred_element_type=F32)


def fold(x, op):
    return op(x.reshape(x.shape[0] // 8, 8, x.shape[1]), axis=0)


Z_OFFSET = (0, 1, -1, 2, -2, 3, -3, 4)


def kernel(
    q_in, k_in, v_in, og_in, w_in,
    dq_out, dk_out, dv_out, dw_out,
    qg, kg, vg, kt, vt, og, ogt, wg, part, part_in, gt, gs,
    s_tile, powers, grads, shift, sums,
    o_send, o_in, l_send, l_in, st_send, st_in,
    xg, att, dq_send, dq_in, dk_send, dk_in, dv_send, dv_in,
    p_send, p_in,
    send, recv, here,
):
    xh = lax.axis_index("tensor_0")
    co = lax.axis_index("tensor_1")
    xl = lax.axis_index("context_0")
    y = lax.axis_index("context_1")
    z = lax.axis_index("context_2")

    def z_to(i):
        return {"context_2": lax.rem(z + Z_OFFSET[i] + 8, 8)}

    def z_back(i):
        return {"context_2": lax.rem(z - Z_OFFSET[i] + 8, 8)}

    def u_to(e):
        return {
            "context_0": lax.rem(xl + e // 4, 2),
            "context_1": lax.rem(y + e % 4, 4),
        }

    def u_back(e):
        return {
            "context_0": lax.rem(xl + e // 4, 2),
            "context_1": lax.rem(y + 4 - e % 4, 4),
        }

    def t_to(s):
        return {
            "tensor_0": lax.rem(xh + s // 2, 2),
            "tensor_1": lax.rem(co + s % 2, 2),
        }

    def w_to(s):
        target = t_to(s)
        if s // 2:
            target["context_0"] = 1 - xl
        return target

    def remote(src, dst, row, slot, target, recv_slot=None):
        return pltpu.make_async_remote_copy(
            src_ref=src,
            dst_ref=dst,
            send_sem=send.at[row, slot],
            recv_sem=recv.at[row, slot if recv_slot is None else recv_slot],
            device_id=target,
            device_id_type=pl.DeviceIdType.MESH,
        )

    def span(e, count=ROWS):
        return slice(e * count, (e + 1) * count)

    tensor_place = 2 * xh + co
    own_rows = [
        pltpu.make_async_copy(og_in, og, here.at[3]),
        pltpu.make_async_copy(
            w_in.at[pl.ds(pl.multiple_of(tensor_place * FEATURES, FEATURES), FEATURES)],
            wg.at[0],
            here.at[4],
        ),
        pltpu.make_async_copy(q_in, qg.at[span(0)], here.at[0]),
        pltpu.make_async_copy(k_in, kg.at[span(0)], here.at[1]),
        pltpu.make_async_copy(v_in, vg.at[span(0)], here.at[2]),
    ]
    for copy in own_rows:
        copy.start()

    barrier = pltpu.get_barrier_semaphore()

    def greet(target):
        pl.semaphore_signal(
            barrier, inc=1, device_id=target, device_id_type=pl.DeviceIdType.MESH
        )

    for i in range(7, 0, -1):
        greet(z_to(i))
        greet(u_to(i))
    for s in range(1, 4):
        greet(w_to(s))
    for copy in own_rows:
        copy.wait()
    for c in range(FEATURES // ROWS):
        ogt[span(c), :] = og[:, span(c)].astype(F32).T.astype(BF16)
    g_sum = dot(og[...], wg[0], 1, 0)
    own_subset = pl.multiple_of((xl * 4 + y) * SUBSET, SUBSET)
    xg[0, :, span(0)] = ogt[pl.ds(own_subset, SUBSET), :]
    pl.semaphore_wait(barrier, 17)

    def q_copy(i):
        source = {5: 3, 7: 3, 6: 4}.get(i, 0)
        target = {5: 1, 7: 3, 6: 2}.get(i, i)
        return remote(qg.at[span(source)], qg.at[span(i)], Q, i, z_to(target))

    def k_copy(e):
        return remote(k_in, kg.at[span(e)], K, e, u_to(e))

    def v_copy(e):
        return remote(v_in, vg.at[span(e)], V, e, u_to(e))

    def w_copy(s):
        place = 2 * lax.rem(xh + s // 2, 2) + lax.rem(co + s % 2, 2)
        block = w_in.at[pl.ds(pl.multiple_of(place * FEATURES, FEATURES), FEATURES)]
        return remote(block, wg.at[s], W, s, w_to(s))

    def x_copy(other, e):
        target = u_to(e)
        place = target["context_0"] * 4 + target["context_1"]
        block = ogt.at[pl.ds(pl.multiple_of(place * SUBSET, SUBSET), SUBSET)]
        if other:
            target["tensor_0"] = 1 - xh
        return remote(block, xg.at[other, :, span(e)], (X, XC)[other], e, target)

    near = (1, 3, 4, 5, 7, 2, 6)
    for i in (3, 4, 1, 2):
        q_copy(i).start()
    for e in near:
        k_copy(e).start()
    for s in (2, 3, 1):
        w_copy(s).start()
    for e in near:
        v_copy(e).start()
    for e in near:
        x_copy(0, e).start()

    q_copy(3).wait_recv()
    q_copy(5).start()
    q_copy(7).start()
    q_copy(4).wait_recv()
    q_copy(6).start()
    for e in near:
        k_copy(e).wait_recv()

    def o_copy(i):
        return remote(o_send.at[i], o_in.at[i], O, i, z_back(i))

    def l_copy(i):
        return remote(l_send.at[i], l_in.at[i], L, i, z_back(i))

    def score(i, j, top):
        scores = dot(kg[span(j), :], qg[span(i), :], 1, 1) * SCORE_SCALE
        s_tile[i % 2, span(j), :] = scores
        highest = fold(scores, jnp.max)
        return highest if top is None else jnp.maximum(top, highest)

    def give(i, weighted, row_total):
        o_send[i] = (weighted / row_total).astype(BF16)
        l_send[i] = jnp.broadcast_to(shift[i] + jnp.log2(row_total), (8, ROWS))
        if i:
            o_copy(i).start()
            l_copy(i).start()

    top = None
    for j in range(8):
        top = score(0, j, top)
    for i in range(8):
        if 3 != i + 1 != 4 and i < 7:
            q_copy(i + 1).wait_recv()
        row_shift = jnp.ceil(jnp.max(top, axis=0, keepdims=True))
        shift[i] = row_shift
        if i == EARLY:
            for e in near:
                v_copy(e).wait_recv()
            for e in range(8):
                vt[:, span(e)] = vg[span(e), :].astype(F32).T.astype(BF16)
            for h in range(EARLY - 1, -1, -1):
                give(h, dot(vt[...], powers[:, span(h)], 1, 0), sums[h])
        top = None
        total = jnp.zeros((8, ROWS), F32)
        weighted = jnp.zeros((HD, ROWS), F32)
        for j in range(8):
            if i < 7:
                top = score(i + 1, j, top)
            p = jnp.exp2(s_tile[i % 2, span(j), :] - row_shift)
            total = total + fold(p, jnp.sum)
            p = p.astype(BF16)
            powers[span(j), span(i)] = p
            if i >= EARLY:
                weighted = weighted + dot(vt[:, span(j)], p, 1, 0)
        row_total = jnp.sum(total, axis=0, keepdims=True)
        if i < EARLY:
            sums[i] = row_total
        else:
            give(i, weighted, row_total)

    def part_copy(s):
        return remote(part.at[s], part_in.at[s], PA, s, t_to(s))

    for s in (1, 2, 3):
        w_copy(s).wait_recv()
        part[s] = dot(og[...], wg[s], 1, 0).astype(BF16)
        part_copy(s).start()
    for e in (0,) + near:
        x_copy(1, e).start()
    for e in range(8):
        kt[:, span(e)] = kg[span(e), :].astype(F32).T.astype(BF16)
    for s in (1, 2, 3):
        part_copy(s).wait_recv()
        g_sum = g_sum + part_in[s].astype(F32)
    g_own = g_sum.T.astype(BF16)
    gt[0] = g_own

    def g_copy(i):
        source = {5: 3, 7: 3, 6: 4}.get(i, 0)
        target = {5: 1, 7: 3, 6: 2}.get(i, i)
        return remote(gt.at[source], gt.at[i], G, i, z_to(target))

    for i in (3, 4, 1, 2):
        g_copy(i).start()

    for i in range(1, 8):
        l_copy(i).wait_recv()
    log_parts = [l_send[0][0:1, :]] + [l_in[i][0:1, :] for i in range(1, 8)]
    highest = log_parts[0]
    for value in log_parts[1:]:
        highest = jnp.maximum(highest, value)
    factors = [jnp.exp2(value - highest) for value in log_parts]
    total = factors[0]
    for value in factors[1:]:
        total = total + value
    joined = (factors[0] / total) * o_send[0].astype(F32)
    for i in range(1, 8):
        o_copy(i).wait_recv()
        joined = joined + (factors[i] / total) * o_in[i].astype(F32)
    attended = joined.astype(BF16)
    att[span(0, HD), span(0)] = attended

    log_total = highest + jnp.log2(total)
    row_delta = jnp.sum(attended.astype(F32) * g_own.astype(F32), axis=0, keepdims=True)
    st_send[0:8, :] = jnp.broadcast_to(log_total, (8, ROWS))
    st_send[8:16, :] = jnp.broadcast_to(row_delta, (8, ROWS))
    st_in[0] = st_send[...]

    def st_copy(i):
        return remote(st_send, st_in.at[i], ST, i, z_to(i))

    for i in range(1, 8):
        st_copy(i).start()

    def a_copy(other, e):
        target = u_to(e)
        if other:
            target["tensor_1"] = 1 - co
        return remote(
            att.at[span(0, HD), span(0)],
            att.at[span(other, HD), span(e)],
            (AT, AC)[other],
            e,
            target,
        )

    for e in (0,) + near:
        if e:
            a_copy(0, e).start()
        a_copy(1, e).start()
    g_copy(3).wait_recv()
    g_copy(5).start()
    g_copy(7).start()
    g_copy(4).wait_recv()
    g_copy(6).start()

    def dq_copy(i):
        return remote(dq_send.at[i], dq_in.at[i], DQ, i, z_back(i))

    for i in range(8):
        if i:
            if 3 != i != 4:
                g_copy(i).wait_recv()
            st_copy(i).wait_recv()
        factor = jnp.exp2(shift[i] - st_in[i, 0:1, :])
        delta = factor * st_in[i, 8:9, :]
        g_block = (gt[i].astype(F32) * factor).astype(BF16)
        gs[:, span(i)] = g_block
        query_sum = jnp.zeros((HD, ROWS), F32)
        for j in range(8):
            prob = dot(vg[span(j), :], g_block, 1, 0)
            slope = ((prob - delta) * powers[span(j), span(i)].astype(F32)).astype(BF16)
            grads[span(j), span(i)] = slope
            query_sum = query_sum + dot(kt[:, span(j)], slope, 1, 0)
        dq_send[i] = query_sum.astype(BF16)
        if i:
            dq_copy(i).start()

    def dk_copy(e):
        return remote(dk_send.at[e], dk_in.at[e], DK, e, u_back(e))

    def dv_copy(e):
        return remote(dv_send.at[e], dv_in.at[e], DV, e, u_back(e))

    def key_side(e):
        dk_send[e] = dot(grads[span(e), :], qg[...], 1, 0).astype(BF16)
        if e:
            dk_copy(e).start()
        dv_send[e] = dot(powers[span(e), :], gs[...], 1, 1).astype(BF16)
        if e:
            dv_copy(e).start()

    for e in (6, 2, 7, 5):
        key_side(e)

    self_served = jnp.logical_and(
        jnp.logical_and(co == lax.div(y, 2), xl == lax.rem(y, 2)), y == lax.div(z, 2)
    )

    def p_copy(n):
        target = {
            "tensor_1": lax.rem(co + n % 2, 2),
            "context_0": lax.rem(xh + n // 4, 2),
            "context_1": 2 * co + xl,
            "context_2": 2 * y + n // 2 % 2,
        }
        return remote(p_send.at[n], p_in.at[z], S2, n, target, z)

    def p_own(n):
        if n % 2:
            return False
        same = jnp.logical_and(lax.rem(xh + n // 4, 2) == xl, lax.rem(z, 2) == n // 2 % 2)
        return jnp.logical_and(self_served, same)

    for e in (0,) + near:
        if e:
            x_copy(0, e).wait_recv()
            a_copy(0, e).wait_recv()
        x_copy(1, e).wait_recv()
        a_copy(1, e).wait_recv()
    for t in range(2):
        product = dot(xg[t], att[...], 1, 1).astype(BF16)
        for r in range(2):
            for c in range(2):
                n = 4 * t + 2 * r + c
                p_send[n] = product[span(r, PIECE), span(c, HD)]
                if c:
                    p_copy(n).start()
                else:
                    @pl.when(jnp.logical_not(p_own(n)))
                    def _(n=n):
                        p_copy(n).start()

                    @pl.when(p_own(n))
                    def _(n=n):
                        p_in[z] = p_send[n]

    for e in (4, 3, 1, 0):
        key_side(e)

    total = dq_send[0].astype(F32)
    for i in range(1, 8):
        dq_copy(i).wait_recv()
        total = total + dq_in[i].astype(F32)
    dq_out[...] = (total * SCALING).T.astype(BF16)
    for n in range(8):
        @pl.when(jnp.logical_not(jnp.logical_and(self_served, z == n)))
        def _(n=n):
            remote(p_send.at[n], p_in.at[n], S2, n, z_to(1)).wait_recv()

    total = p_in[0].astype(F32)
    for n in range(1, 8):
        total = total + p_in[n].astype(F32)
    dw_out[...] = total
    total = dk_send[0].astype(F32)
    for e in range(1, 8):
        dk_copy(e).wait_recv()
        total = total + dk_in[e].astype(F32)
    dk_out[...] = (total * SCALING).astype(BF16)
    total = dv_send[0].astype(F32)
    for e in range(1, 8):
        dv_copy(e).wait_recv()
        total = total + dv_in[e].astype(F32)
    dv_out[...] = total.astype(BF16)

    for i in range(1, 8):
        for copy in (q_copy, k_copy, v_copy, g_copy, o_copy, l_copy, st_copy, dq_copy, dk_copy,
                     dv_copy):
            copy(i).wait_send()
        x_copy(0, i).wait_send()
        a_copy(0, i).wait_send()
    for i in range(8):
        x_copy(1, i).wait_send()
        a_copy(1, i).wait_send()
    for s in range(1, 4):
        w_copy(s).wait_send()
        part_copy(s).wait_send()
    for n in range(8):
        if n % 2:
            p_copy(n).wait_send()
        else:
            @pl.when(jnp.logical_not(p_own(n)))
            def _(n=n):
                p_copy(n).wait_send()


def hand_over(*refs):
    for source, target in zip(refs[:4], refs[4:]):
        target[...] = source[...]


def local(q, k, v, og, w):
    anywhere = pl.BlockSpec(memory_space=pl.ANY)
    vmem = pl.BlockSpec(memory_space=pltpu.VMEM)
    tokens = 8 * ROWS
    block = (8, ROWS, HD)
    turned = (8, HD, ROWS)
    shapes = (
        jax.ShapeDtypeStruct((ROWS, HD), BF16),
        jax.ShapeDtypeStruct((ROWS, HD), BF16),
        jax.ShapeDtypeStruct((ROWS, HD), BF16),
        jax.ShapeDtypeStruct((PIECE, HD), F32),
    )
    results = pl.pallas_call(
        kernel,
        out_shape=shapes,
        in_specs=[anywhere] * 5,
        out_specs=(vmem,) * 4,
        scratch_shapes=[
            pltpu.VMEM((tokens, HD), BF16),
            pltpu.VMEM((tokens, HD), BF16),
            pltpu.VMEM((tokens, HD), BF16),
            pltpu.VMEM((HD, tokens), BF16),
            pltpu.VMEM((HD, tokens), BF16),
            pltpu.VMEM((ROWS, FEATURES), BF16),
            pltpu.VMEM((FEATURES, ROWS), BF16),
            pltpu.VMEM((4, FEATURES, HD), BF16),
            pltpu.VMEM((4, ROWS, HD), BF16),
            pltpu.VMEM((4, ROWS, HD), BF16),
            pltpu.VMEM(turned, BF16),
            pltpu.VMEM((HD, tokens), BF16),
            pltpu.VMEM((2, tokens, ROWS), F32),
            pltpu.VMEM((tokens, tokens), BF16),
            pltpu.VMEM((tokens, tokens), BF16),
            pltpu.VMEM((8, 1, ROWS), F32),
            pltpu.VMEM((8, 1, ROWS), F32),
            pltpu.VMEM(turned, BF16),
            pltpu.VMEM(turned, BF16),
            pltpu.VMEM((8, 8, ROWS), F32),
            pltpu.VMEM((8, 8, ROWS), F32),
            pltpu.VMEM((16, ROWS), F32),
            pltpu.VMEM((8, 16, ROWS), F32),
            pltpu.VMEM((2, SUBSET, tokens), BF16),
            pltpu.VMEM((2 * HD, tokens), BF16),
            pltpu.VMEM(turned, BF16),
            pltpu.VMEM(turned, BF16),
            pltpu.VMEM(block, BF16),
            pltpu.VMEM(block, BF16),
            pltpu.VMEM(block, BF16),
            pltpu.VMEM(block, BF16),
            pltpu.VMEM((8, PIECE, HD), BF16),
            pltpu.VMEM((8, PIECE, HD), BF16),
            pltpu.SemaphoreType.DMA((17, 8)),
            pltpu.SemaphoreType.DMA((17, 8)),
            pltpu.SemaphoreType.DMA((5,)),
        ],
        compiler_params=pltpu.CompilerParams(
            collective_id=0,
            has_side_effects=True,
            vmem_limit_bytes=56 * 1024 * 1024,
        ),
    )(q, k, v, og, w)
    return pl.pallas_call(
        hand_over,
        out_shape=shapes,
        in_specs=[vmem] * 4,
        out_specs=(vmem,) * 4,
    )(*results)


def solution(mesh):
    torus = Mesh(mesh.devices.reshape(2, 2, 2, 4, 8), TENSOR + CONTEXT)
    tiles = P(CONTEXT, TENSOR)
    return jax.shard_map(
        local,
        mesh=torus,
        in_specs=(tiles, tiles, tiles, tiles, P(None, TENSOR)),
        out_specs=(tiles, tiles, tiles, tiles),
        check_vma=False,
    )
```

time: 96.6 us -> 86.2 us (0.89)
  the two profiles are of different devices: /device:TPU:1 before, /device:TPU:35 now
where the time goes in v2:
time: 86.2 us; the launch traced here: 86 us
  Pallas kernels  85.4 us (99%)
    pallas_call x1, Pallas kernels, local(): pl.pallas_call(kernel, out_shape=shapes, in_specs=[anywhere] * 5, out_spe...  83.8 us

profile of v2, /device:TPU:35, one launch (start us, length us, event | category | flops | bytes accessed | tf_op | source)
XLA Modules:
  0.0 86.0 jit_solution(11156264731635424263)
XLA Ops:
  0.6 83.8 %shard_map.84 = (bf16[256,128]{1,0:T(8,128)(2,1)}, bf16[256,128]{1,0:T(8,128)(2,1)}, bf16[256,128]{1,0:T(8,128)(2,1)}, f32[96,128]{1,0:T(8,128)}) custom-call(bf16[256,128]{1,0:T(8,128)(2,1)} %q_in.1, bf16[256,128]{1,0:T(8,128)(2,1)} %k_in.1, bf16[256,128]{1,0:T(8,128)(2,1)} %v_in.1, bf16[256,1536]{1,0:T(8,128)(2,1)} %og_in.1, bf16[6144,128]{1,0:T(8,128)(2,1)} %w_in.1), custom_call_target="tpu_custom_call" | custom-call | tf_op jit(solution)/shard_map/pallas_call | solution.py:451
  84.4 1.6 %shard_map.85 = (bf16[256,128]{1,0:T(8,128)(2,1)}, bf16[256,128]{1,0:T(8,128)(2,1)}, bf16[256,128]{1,0:T(8,128)(2,1)}, f32[96,128]{1,0:T(8,128)}) custom-call(bf16[256,128]{1,0:T(8,128)(2,1)} %get-tuple-element.8.refs_0_, bf16[256,128]{1,0:T(8,128)(2,1)} %get-tuple-element.9.refs_1_, bf16[256,128]{1,0:T(8,128)(2,1)} %get-tuple-element.10.refs_2_, ...), custom_call_target="tpu_custom_call" | custom-call | tf_op jit(solution)/shard_map/pallas_call | solution.py:500

commit v3 on v2

--- a/solution.py
+++ b/solution.py
@@ -93,6 +93,9 @@
     def span(e, count=ROWS):
         return slice(e * count, (e + 1) * count)
 
+    def pair(row, half):
+        return lax.rem(row + lax.div(z, 2) + 2 * half, 4)
+
     tensor_place = 2 * xh + co
     own_rows = [
         pltpu.make_async_copy(og_in, og, here.at[3]),
@@ -125,7 +128,7 @@
     for c in range(FEATURES // ROWS):
         ogt[span(c), :] = og[:, span(c)].astype(F32).T.astype(BF16)
     g_sum = dot(og[...], wg[0], 1, 0)
-    own_subset = pl.multiple_of((xl * 4 + y) * SUBSET, SUBSET)
+    own_subset = pl.multiple_of((xl * 4 + pair(y, xh)) * SUBSET, SUBSET)
     xg[0, :, span(0)] = ogt[pl.ds(own_subset, SUBSET), :]
     pl.semaphore_wait(barrier, 17)
 
@@ -145,13 +148,21 @@
         block = w_in.at[pl.ds(pl.multiple_of(place * FEATURES, FEATURES), FEATURES)]
         return remote(block, wg.at[s], W, s, w_to(s))
 
-    def x_copy(other, e):
+    def x_copy(e):
         target = u_to(e)
-        place = target["context_0"] * 4 + target["context_1"]
+        place = target["context_0"] * 4 + pair(target["context_1"], xh)
         block = ogt.at[pl.ds(pl.multiple_of(place * SUBSET, SUBSET), SUBSET)]
-        if other:
-            target["tensor_0"] = 1 - xh
-        return remote(block, xg.at[other, :, span(e)], (X, XC)[other], e, target)
+        return remote(block, xg.at[0, :, span(e)], X, e, target)
+
+    def x_pass(half):
+        return remote(
+            xg.at[0, :, span(half, 4 * ROWS)],
+            xg.at[1, :, span(1 - half, 4 * ROWS)],
+            XC,
+            half,
+            w_to(2),
+            1 - half,
+        )
 
     near = (1, 3, 4, 5, 7, 2, 6)
     for i in (3, 4, 1, 2):
@@ -163,7 +174,7 @@
     for e in near:
         v_copy(e).start()
     for e in near:
-        x_copy(0, e).start()
+        x_copy(e).start()
 
     q_copy(3).wait_recv()
     q_copy(5).start()
@@ -232,8 +243,10 @@
         w_copy(s).wait_recv()
         part[s] = dot(og[...], wg[s], 1, 0).astype(BF16)
         part_copy(s).start()
-    for e in (0,) + near:
-        x_copy(1, e).start()
+    for e in near:
+        x_copy(e).wait_recv()
+    for half in range(2):
+        x_pass(half).start()
     for e in range(8):
         kt[:, span(e)] = kg[span(e), :].astype(F32).T.astype(BF16)
     for s in (1, 2, 3):
@@ -279,22 +292,15 @@
     for i in range(1, 8):
         st_copy(i).start()
 
-    def a_copy(other, e):
-        target = u_to(e)
-        if other:
-            target["tensor_1"] = 1 - co
-        return remote(
-            att.at[span(0, HD), span(0)],
-            att.at[span(other, HD), span(e)],
-            (AT, AC)[other],
-            e,
-            target,
-        )
-
-    for e in (0,) + near:
-        if e:
-            a_copy(0, e).start()
-        a_copy(1, e).start()
+    def a_copy(e):
+        own = att.at[span(0, HD), span(0)]
+        return remote(own, att.at[span(0, HD), span(e)], AT, e, u_to(e))
+
+    def a_pass():
+        return remote(att.at[span(0, HD)], att.at[span(1, HD)], AC, 0, t_to(1))
+
+    for e in near:
+        a_copy(e).start()
     g_copy(3).wait_recv()
     g_copy(5).start()
     g_copy(7).start()
@@ -304,15 +310,18 @@
     def dq_copy(i):
         return remote(dq_send.at[i], dq_in.at[i], DQ, i, z_back(i))
 
-    for i in range(8):
+    def weigh(i):
         if i:
             if 3 != i != 4:
                 g_copy(i).wait_recv()
             st_copy(i).wait_recv()
         factor = jnp.exp2(shift[i] - st_in[i, 0:1, :])
-        delta = factor * st_in[i, 8:9, :]
-        g_block = (gt[i].astype(F32) * factor).astype(BF16)
-        gs[:, span(i)] = g_block
+        sums[i] = factor * st_in[i, 8:9, :]
+        gs[:, span(i)] = (gt[i].astype(F32) * factor).astype(BF16)
+
+    def query_side(i):
+        delta = sums[i]
+        g_block = gs[:, span(i)]
         query_sum = jnp.zeros((HD, ROWS), F32)
         for j in range(8):
             prob = dot(vg[span(j), :], g_block, 1, 0)
@@ -329,27 +338,31 @@
     def dv_copy(e):
         return remote(dv_send.at[e], dv_in.at[e], DV, e, u_back(e))
 
-    def key_side(e):
-        dk_send[e] = dot(grads[span(e), :], qg[...], 1, 0).astype(BF16)
-        if e:
-            dk_copy(e).start()
+    for i in (1, 2, 0, 3):
+        weigh(i)
+        query_side(i)
+    for i in range(4, 8):
+        weigh(i)
+    for e in (6, 2, 7, 5, 4, 3, 1, 0):
         dv_send[e] = dot(powers[span(e), :], gs[...], 1, 1).astype(BF16)
         if e:
             dv_copy(e).start()
-
-    for e in (6, 2, 7, 5):
-        key_side(e)
+    for e in near:
+        a_copy(e).wait_recv()
+    a_pass().start()
+    for i in (7, 5, 6, 4):
+        query_side(i)
 
     self_served = jnp.logical_and(
-        jnp.logical_and(co == lax.div(y, 2), xl == lax.rem(y, 2)), y == lax.div(z, 2)
+        jnp.logical_and(co == lax.div(y, 2), xh == lax.rem(y, 2)), y == 2 * xl
     )
 
     def p_copy(n):
         target = {
             "tensor_1": lax.rem(co + n % 2, 2),
             "context_0": lax.rem(xh + n // 4, 2),
-            "context_1": 2 * co + xl,
-            "context_2": 2 * y + n // 2 % 2,
+            "context_1": 2 * co + lax.rem(xl + n // 4, 2),
+            "context_2": 2 * pair(y, lax.rem(xh + n // 4, 2)) + n // 2 % 2,
         }
         return remote(p_send.at[n], p_in.at[z], S2, n, target, z)
 
@@ -359,12 +372,9 @@
         same = jnp.logical_and(lax.rem(xh + n // 4, 2) == xl, lax.rem(z, 2) == n // 2 % 2)
         return jnp.logical_and(self_served, same)
 
-    for e in (0,) + near:
-        if e:
-            x_copy(0, e).wait_recv()
-            a_copy(0, e).wait_recv()
-        x_copy(1, e).wait_recv()
-        a_copy(1, e).wait_recv()
+    for half in range(2):
+        x_pass(half).wait_recv()
+    a_pass().wait_recv()
     for t in range(2):
         product = dot(xg[t], att[...], 1, 1).astype(BF16)
         for r in range(2):
@@ -382,9 +392,16 @@
                     def _(n=n):
                         p_in[z] = p_send[n]
 
-    for e in (4, 3, 1, 0):
-        key_side(e)
-
+    for e in (6, 2, 7, 5, 4, 3, 1, 0):
+        dk_send[e] = dot(grads[span(e), :], qg[...], 1, 0).astype(BF16)
+        if e:
+            dk_copy(e).start()
+
+    total = dv_send[0].astype(F32)
+    for e in range(1, 8):
+        dv_copy(e).wait_recv()
+        total = total + dv_in[e].astype(F32)
+    dv_out[...] = total.astype(BF16)
     total = dq_send[0].astype(F32)
     for i in range(1, 8):
         dq_copy(i).wait_recv()
@@ -404,21 +421,16 @@
         dk_copy(e).wait_recv()
         total = total + dk_in[e].astype(F32)
     dk_out[...] = (total * SCALING).astype(BF16)
-    total = dv_send[0].astype(F32)
-    for e in range(1, 8):
-        dv_copy(e).wait_recv()
-        total = total + dv_in[e].astype(F32)
-    dv_out[...] = total.astype(BF16)
 
     for i in range(1, 8):
         for copy in (q_copy, k_copy, v_copy, g_copy, o_copy, l_copy, st_copy, dq_copy, dk_copy,
                      dv_copy):
             copy(i).wait_send()
-        x_copy(0, i).wait_send()
-        a_copy(0, i).wait_send()
-    for i in range(8):
-        x_copy(1, i).wait_send()
-        a_copy(1, i).wait_send()
+        x_copy(i).wait_send()
+        a_copy(i).wait_send()
+    a_pass().wait_send()
+    for half in range(2):
+        x_pass(half).wait_send()
     for s in range(1, 4):
         w_copy(s).wait_send()
         part_copy(s).wait_send()

time: 86.2 us -> 76.4 us (0.89)
  the two profiles are of different devices: /device:TPU:35 before, /device:TPU:1 now
where the time goes in v3:
time: 76.4 us; the launch traced here: 76.2 us
  Pallas kernels  75.6 us (99%)
    pallas_call x1, Pallas kernels, local(): pl.pallas_call(kernel, out_shape=shapes, in_specs=[anywhere] * 5, out_spe...  74 us
    pallas_call x1, Pallas kernels, local(): pl.pallas_call(hand_over, out_shape=shapes, in_specs=[vmem] * 4, out_spec...  1.6 us

profile of v3, /device:TPU:1, one launch (start us, length us, event | category | flops | bytes accessed | tf_op | source)
XLA Modules:
  0.0 76.2 jit_solution(17294069274533633780)
XLA Ops:
  0.6 74.0 %shard_map.84 = (bf16[256,128]{1,0:T(8,128)(2,1)}, bf16[256,128]{1,0:T(8,128)(2,1)}, bf16[256,128]{1,0:T(8,128)(2,1)}, f32[96,128]{1,0:T(8,128)}) custom-call(bf16[256,128]{1,0:T(8,128)(2,1)} %q_in.1, bf16[256,128]{1,0:T(8,128)(2,1)} %k_in.1, bf16[256,128]{1,0:T(8,128)(2,1)} %v_in.1, bf16[256,1536]{1,0:T(8,128)(2,1)} %og_in.1, bf16[6144,128]{1,0:T(8,128)(2,1)} %w_in.1), custom_call_target="tpu_custom_call" | custom-call | tf_op jit(solution)/shard_map/pallas_call | solution.py:463
  74.6 1.6 %shard_map.85 = (bf16[256,128]{1,0:T(8,128)(2,1)}, bf16[256,128]{1,0:T(8,128)(2,1)}, bf16[256,128]{1,0:T(8,128)(2,1)}, f32[96,128]{1,0:T(8,128)}) custom-call(bf16[256,128]{1,0:T(8,128)(2,1)} %get-tuple-element.8.refs_0_, bf16[256,128]{1,0:T(8,128)(2,1)} %get-tuple-element.9.refs_1_, bf16[256,128]{1,0:T(8,128)(2,1)} %get-tuple-element.10.refs_2_, ...), custom_call_target="tpu_custom_call" | custom-call | tf_op jit(solution)/shard_map/pallas_call | solution.py:512

commit v4 on v3

--- a/solution.py
+++ b/solution.py
@@ -19,7 +19,7 @@
 F32 = jnp.float32
 
 (Q, K, V, G, O, L, ST, DQ, DK, DV, W, PA, X, XC, AT, AC, S2) = range(17)
-EARLY = 6
+EARLY = 3
 SUBSET = 192
 
 
@@ -138,10 +138,14 @@
         return remote(qg.at[span(source)], qg.at[span(i)], Q, i, z_to(target))
 
     def k_copy(e):
-        return remote(k_in, kg.at[span(e)], K, e, u_to(e))
+        if e > 4:
+            return remote(kg.at[span(e - 4)], kg.at[span(e)], K, e, u_to(4))
+        return remote(kg.at[span(0)], kg.at[span(e)], K, e, u_to(e))
 
     def v_copy(e):
-        return remote(v_in, vg.at[span(e)], V, e, u_to(e))
+        if e > 4:
+            return remote(vg.at[span(4)], vg.at[span(e)], V, e, u_to(e - 4))
+        return remote(vg.at[span(0)], vg.at[span(e)], V, e, u_to(e))
 
     def w_copy(s):
         place = 2 * lax.rem(xh + s // 2, 2) + lax.rem(co + s % 2, 2)
@@ -165,23 +169,33 @@
         )
 
     near = (1, 3, 4, 5, 7, 2, 6)
+    for e in (1, 3, 4):
+        k_copy(e).start()
     for i in (3, 4, 1, 2):
         q_copy(i).start()
-    for e in near:
-        k_copy(e).start()
+    v_copy(4).start()
+    k_copy(2).start()
     for s in (2, 3, 1):
         w_copy(s).start()
-    for e in near:
+    for e in (1, 3, 2):
         v_copy(e).start()
-    for e in near:
-        x_copy(e).start()
-
+
+    for e in (1, 3):
+        k_copy(e).wait_recv()
+        k_copy(e + 4).start()
     q_copy(3).wait_recv()
     q_copy(5).start()
     q_copy(7).start()
     q_copy(4).wait_recv()
     q_copy(6).start()
+    k_copy(2).wait_recv()
+    k_copy(6).start()
+    v_copy(4).wait_recv()
+    for e in (5, 7, 6):
+        v_copy(e).start()
     for e in near:
+        x_copy(e).start()
+    for e in (4, 5, 7, 6):
         k_copy(e).wait_recv()
 
     def o_copy(i):
@@ -212,7 +226,7 @@
         row_shift = jnp.ceil(jnp.max(top, axis=0, keepdims=True))
         shift[i] = row_shift
         if i == EARLY:
-            for e in near:
+            for e in (1, 3, 2, 5, 7, 6):
                 v_copy(e).wait_recv()
             for e in range(8):
                 vt[:, span(e)] = vg[span(e), :].astype(F32).T.astype(BF16)
@@ -243,10 +257,6 @@
         w_copy(s).wait_recv()
         part[s] = dot(og[...], wg[s], 1, 0).astype(BF16)
         part_copy(s).start()
-    for e in near:
-        x_copy(e).wait_recv()
-    for half in range(2):
-        x_pass(half).start()
     for e in range(8):
         kt[:, span(e)] = kg[span(e), :].astype(F32).T.astype(BF16)
     for s in (1, 2, 3):
@@ -262,6 +272,10 @@
 
     for i in (3, 4, 1, 2):
         g_copy(i).start()
+    for e in near:
+        x_copy(e).wait_recv()
+    for half in range(2):
+        x_pass(half).start()
 
     for i in range(1, 8):
         l_copy(i).wait_recv()
@@ -282,8 +296,8 @@
 
     log_total = highest + jnp.log2(total)
     row_delta = jnp.sum(attended.astype(F32) * g_own.astype(F32), axis=0, keepdims=True)
-    st_send[0:8, :] = jnp.broadcast_to(log_total, (8, ROWS))
-    st_send[8:16, :] = jnp.broadcast_to(row_delta, (8, ROWS))
+    upper = lax.broadcasted_iota(jnp.int32, (8, ROWS), 0) < 4
+    st_send[...] = jnp.where(upper, log_total, row_delta)
     st_in[0] = st_send[...]
 
     def st_copy(i):
@@ -316,7 +330,7 @@
                 g_copy(i).wait_recv()
             st_copy(i).wait_recv()
         factor = jnp.exp2(shift[i] - st_in[i, 0:1, :])
-        sums[i] = factor * st_in[i, 8:9, :]
+        sums[i] = factor * st_in[i, 4:5, :]
         gs[:, span(i)] = (gt[i].astype(F32) * factor).astype(BF16)
 
     def query_side(i):
@@ -487,8 +501,8 @@
             pltpu.VMEM(turned, BF16),
             pltpu.VMEM((8, 8, ROWS), F32),
             pltpu.VMEM((8, 8, ROWS), F32),
-            pltpu.VMEM((16, ROWS), F32),
-            pltpu.VMEM((8, 16, ROWS), F32),
+            pltpu.VMEM((8, ROWS), F32),
+            pltpu.VMEM((8, 8, ROWS), F32),
             pltpu.VMEM((2, SUBSET, tokens), BF16),
             pltpu.VMEM((2 * HD, tokens), BF16),
             pltpu.VMEM(turned, BF16),

time: 76.4 us -> 74.8 us (0.979)
  Pallas kernels: 75.6 us -> 74 us
    pallas_call x1, Pallas kernels: 74 us -> 72.4 us  [local(): pl.pallas_call(kernel, out_shape=shapes, in_specs=[anywhere] * 5, out_spe...]
where the time goes in v4:
time: 74.8 us; the launch traced here: 74.7 us
  Pallas kernels  74 us (99%)
    pallas_call x1, Pallas kernels, local(): pl.pallas_call(kernel, out_shape=shapes, in_specs=[anywhere] * 5, out_spe...  72.4 us
    pallas_call x1, Pallas kernels, local(): pl.pallas_call(hand_over, out_shape=shapes, in_specs=[vmem] * 4, out_spec...  1.6 us

profile of v4, /device:TPU:1, one launch (start us, length us, event | category | flops | bytes accessed | tf_op | source)
XLA Modules:
  0.0 74.7 jit_solution(18284994629659934003)
XLA Ops:
  0.6 72.4 %shard_map.84 = (bf16[256,128]{1,0:T(8,128)(2,1)}, bf16[256,128]{1,0:T(8,128)(2,1)}, bf16[256,128]{1,0:T(8,128)(2,1)}, f32[96,128]{1,0:T(8,128)}) custom-call(bf16[256,128]{1,0:T(8,128)(2,1)} %q_in.1, bf16[256,128]{1,0:T(8,128)(2,1)} %k_in.1, bf16[256,128]{1,0:T(8,128)(2,1)} %v_in.1, bf16[256,1536]{1,0:T(8,128)(2,1)} %og_in.1, bf16[6144,128]{1,0:T(8,128)(2,1)} %w_in.1), custom_call_target="tpu_custom_call" | custom-call | tf_op jit(solution)/shard_map/pallas_call | solution.py:477
  73.1 1.6 %shard_map.85 = (bf16[256,128]{1,0:T(8,128)(2,1)}, bf16[256,128]{1,0:T(8,128)(2,1)}, bf16[256,128]{1,0:T(8,128)(2,1)}, f32[96,128]{1,0:T(8,128)}) custom-call(bf16[256,128]{1,0:T(8,128)(2,1)} %get-tuple-element.8.refs_0_, bf16[256,128]{1,0:T(8,128)(2,1)} %get-tuple-element.9.refs_1_, bf16[256,128]{1,0:T(8,128)(2,1)} %get-tuple-element.10.refs_2_, ...), custom_call_target="tpu_custom_call" | custom-call | tf_op jit(solution)/shard_map/pallas_call | solution.py:526
